TPU v7x, 32 devices: a whole 2x2x4 slice. The times are simulated.
32 devices in a mesh: ctx: 8 (over z, x), head: 4 (over y, core).
Axes of the slice: x: 2, y: 2, z: 4, core: 2. Of those that a mesh axis runs over, the one named last changes fastest.
Arguments:
- queries: bfloat16 [1024, 4096], P('ctx', 'head'), may hold values from -24 to 24
- key_rows: bfloat16 [1024, 4096], P('ctx', 'head'), may hold values from -24 to 24
- value_rows: bfloat16 [1024, 4096], P('ctx', 'head'), may hold values from -6 to 6
- upstream: bfloat16 [1024, 6144], P('ctx', 'head'), may hold values from -6 to 6
- out_weight: bfloat16 [6144, 4096], P('ctx', 'head'), may hold values from -0.078125 to 0.078125
- group_ids: int32 [1024], replicated, may hold values from 0 to 7, never falling along the last dimension, each value on 1 to 256 neighbouring positions
Outputs:
- grad_queries: bfloat16 [1024, 4096], P('ctx', 'head')
- grad_keys: bfloat16 [1024, 4096], P('ctx', 'head')
- grad_values: bfloat16 [1024, 4096], P('ctx', 'head')
Inputs may be any that keep to these rules, and one draw needn't show every extreme that they name: `group_ids`: never falling along the tokens; each group number covers 1 to 256 consecutive tokens, one exactly 256.
All inputs are finite; a program needn't handle non-finite values.
Results may differ from a plain program's by a relative error of at most 0.025.
Values may be sent and summed in bfloat16 or wider, within the bound.
No kernel may reach another device: no remote copies, remote signals or barrier semaphores. Data moves between devices by JAX's collectives and lax.ppermute only.
A program may use at most 64 MiB of HBM per device.

v0:
```python
import jax
import jax.numpy as jnp
from jax import lax
from jax.sharding import PartitionSpec as P

HDIM = 128
masked_score = -1e30


def body(queries, key_rows, value_rows, upstream, out_weight, group_ids):
    rows_dev = queries.shape[0]
    heads_dev = queries.shape[1] // HDIM
    scaling = HDIM ** (-0.5)
    own_start = lax.axis_index("ctx") * rows_dev
    own_ids = lax.dynamic_slice_in_dim(group_ids, own_start, rows_dev, 0)
    upstream_full = lax.all_gather(upstream, "head", axis=1, tiled=True)
    grad_out = jnp.dot(
        upstream_full,
        lax.all_gather(out_weight, "ctx", axis=0, tiled=True),
        preferred_element_type=jnp.float32,
    ).astype(jnp.bfloat16)
    query_heads = queries.reshape(rows_dev, heads_dev, HDIM)
    grad_heads = grad_out.reshape(rows_dev, heads_dev, HDIM)
    key_heads = key_rows.reshape(rows_dev, heads_dev, HDIM)
    value_heads = value_rows.reshape(rows_dev, heads_dev, HDIM)
    stats_shape = (heads_dev, rows_dev)
    key_piece = lax.all_gather(key_rows, "ctx", axis=0, tiled=True)
    piece_rows = key_piece.shape[0]
    piece_ids = group_ids
    key_block = key_piece.reshape(piece_rows, heads_dev, HDIM)
    allowed = (piece_ids[None, :] <= own_ids[:, None])[None]
    run_max = jnp.full(stats_shape, masked_score, jnp.float32)
    scores = scaling * jnp.einsum(
        "qhd,khd->hqk", query_heads, key_block, preferred_element_type=jnp.float32
    )
    scores = jnp.where(allowed, scores, masked_score)
    new_max = jnp.maximum(run_max, jnp.max(scores, axis=2))
    weights = jnp.where(allowed, jnp.exp(scores - new_max[:, :, None]), 0.0)
    run_sum = jnp.sum(weights, axis=2)
    run_max, run_sum = (new_max, run_sum)
    log_total = run_max + jnp.log(run_sum)
    key_piece = lax.all_gather(key_rows, "ctx", axis=0, tiled=True)
    value_piece = lax.all_gather(value_rows, "ctx", axis=0, tiled=True)
    piece_rows = key_piece.shape[0]
    piece_ids = group_ids
    key_block = key_piece.reshape(piece_rows, heads_dev, HDIM)
    value_block = value_piece.reshape(piece_rows, heads_dev, HDIM)
    allowed = (piece_ids[None, :] <= own_ids[:, None])[None]
    scores = scaling * jnp.einsum(
        "qhd,khd->hqk", query_heads, key_block, preferred_element_type=jnp.float32
    )
    probs = jnp.where(allowed, jnp.exp(scores - log_total[:, :, None]), 0.0)
    probs_low = probs.astype(jnp.bfloat16)
    grad_probs = jnp.einsum(
        "qhd,khd->hqk", grad_heads, value_block, preferred_element_type=jnp.float32
    )
    mixed_low = (probs * grad_probs).astype(jnp.bfloat16)
    out_acc = jnp.einsum("hqk,khd->hqd", probs_low, value_block, preferred_element_type=jnp.float32)
    mixed_acc = jnp.einsum("hqk,khd->hqd", mixed_low, key_block, preferred_element_type=jnp.float32)
    plain_acc = jnp.einsum("hqk,khd->hqd", probs_low, key_block, preferred_element_type=jnp.float32)
    forward = (out_acc, mixed_acc, plain_acc)
    attn_out, mixed_acc, plain_acc = forward
    delta = jnp.einsum("qhd,hqd->hq", grad_heads.astype(jnp.float32), attn_out)
    grad_query = scaling * (mixed_acc - delta[:, :, None] * plain_acc)
    grad_queries = (
        grad_query.transpose(1, 0, 2).reshape(rows_dev, heads_dev * HDIM).astype(jnp.bfloat16)
    )
    all_lse, all_delta = (
        lax.all_gather(log_total.T, "ctx", axis=0, tiled=True),
        lax.all_gather(delta.T, "ctx", axis=0, tiled=True),
    )
    query_piece = lax.all_gather(queries, "ctx", axis=0, tiled=True)
    grad_piece = lax.all_gather(grad_out, "ctx", axis=0, tiled=True)
    piece_rows = query_piece.shape[0]
    piece_ids = group_ids
    piece_lse = all_lse.T
    piece_delta = all_delta.T
    query_block = query_piece.reshape(piece_rows, heads_dev, HDIM)
    grad_block = grad_piece.reshape(piece_rows, heads_dev, HDIM)
    allowed = (own_ids[None, :] <= piece_ids[:, None])[None]
    scores = scaling * jnp.einsum(
        "qhd,khd->hqk", query_block, key_heads, preferred_element_type=jnp.float32
    )
    probs = jnp.where(allowed, jnp.exp(scores - piece_lse[:, :, None]), 0.0)
    probs_low = probs.astype(jnp.bfloat16)
    grad_probs = jnp.einsum(
        "qhd,khd->hqk", grad_block, value_heads, preferred_element_type=jnp.float32
    )
    grad_scores = (probs * (grad_probs - piece_delta[:, :, None])).astype(jnp.bfloat16)
    value_grad = jnp.einsum(
        "hqk,qhd->hkd", probs_low, grad_block, preferred_element_type=jnp.float32
    )
    key_grad = jnp.einsum(
        "hqk,qhd->hkd", grad_scores, query_block, preferred_element_type=jnp.float32
    )
    key_grad, value_grad = (key_grad, value_grad)
    grad_keys = (
        (scaling * key_grad)
        .transpose(1, 0, 2)
        .reshape(rows_dev, heads_dev * HDIM)
        .astype(jnp.bfloat16)
    )
    grad_values = (
        value_grad.transpose(1, 0, 2).reshape(rows_dev, heads_dev * HDIM).astype(jnp.bfloat16)
    )
    return (grad_queries, grad_keys, grad_values)


def solution(mesh):
    in_specs = (
        P("ctx", "head"),
        P("ctx", "head"),
        P("ctx", "head"),
        P("ctx", "head"),
        P("ctx", "head"),
        P(),
    )
    out_specs = (P("ctx", "head"), P("ctx", "head"), P("ctx", "head"))
    return jax.shard_map(body, mesh=mesh, in_specs=in_specs, out_specs=out_specs, check_vma=False)
```

profile of v0, /device:TPU:0, one launch (start us, length us, event | category | flops | bytes accessed | tf_op | source)
XLA Modules:
  0.0 434.6 jit_solution(9773748842374155028)
XLA Ops:
  7.2 0.7 all-gather.9.cloned.1.call-update
  8.0 0.7 all-gather.11.cloned.1.call-update
  8.7 1.8 copy.18
  10.6 1.8 copy.21
  12.4 0.5 all-gather.13.cloned.1.call-update
  13.0 1.1 copy.41
  14.2 0.1 dynamic_slice.3
  14.2 0.1 broadcast_compare_fusion.1
  14.4 17.5 %all-gather.9.cloned.1.call-done = bf16[128,6144]{1,0:T(8,128)(2,1)} async-done(((bf16[128,1536]{1,0:T(8,128)(2,1)}), bf16[128,6144]{1,0:T(8,128)(2,1)}) %all-gather.9.cloned.1.call-update) | async-done | bytes 1572880 | tf_op jit(solution)/shard_map/all_gather | solution.py:16
  31.9 178.3 %all-gather.11.cloned.1.call-done = bf16[6144,1024]{1,0:T(8,128)(2,1)} async-done(((bf16[768,1024]{1,0:T(8,128)(2,1)}), bf16[6144,1024]{1,0:T(8,128)(2,1)}) %all-gather.11.cloned.1.call-update) | async-done | bytes 12582928 | tf_op jit(solution)/shard_map/all_gather | solution.py:19
  210.2 7.6 %convolution_convert_fusion = bf16[128,1024]{1,0:T(8,128)(2,1)} fusion(bf16[128,6144]{1,0:T(8,128)(2,1)} %all-gather.9.cloned.1.call-done, bf16[6144,1024]{1,0:T(8,128)(2,1)} %all-gather.11.cloned.1.call-done), kind=kOutput, calls=%fused_computation.28 | convolution fusion | flops 1610743808 | bytes 14417920 | tf_op jit(solution)/shard_map/dot_general | solution.py:17
  217.8 0.2 broadcast_compare_fusion
  218.0 43.4 %all-gather.7.cloned.1.call-done = bf16[1024,1024]{0,1:T(8,128)(2,1)} async-done(((bf16[128,1024]{0,1:T(8,128)(2,1)}), bf16[1024,1024]{0,1:T(8,128)(2,1)}) %all-gather.7.cloned.1.call-update) | async-done | bytes 2097168 | tf_op jit(solution)/shard_map/all_gather | solution.py:42
  261.4 2.7 select_reduce_fusion.1
  264.2 2.0 copy-done
  266.2 1.3 select_reduce_fusion
  267.5 31.1 %all_gather.30 = f32[1024,8]{0,1:T(8,128)S(1)} all-gather(f32[128,8]{0,1:T(8,128)S(1)} %bitcast.100), channel_id=1, replica_groups=mesh['ctx'=8,'head'=4] {'ctx'}, dimensions={0}, use_global_device_ids=true | all-gather | bytes 36864 | tf_op jit(solution)/shard_map/all_gather | solution.py:69
  298.6 13.9 %all-gather.15.cloned.1.call-done = bf16[1024,1024]{0,1:T(8,128)(2,1)} async-done(((bf16[128,1024]{0,1:T(8,128)(2,1)}), bf16[1024,1024]{0,1:T(8,128)(2,1)}) %all-gather.15.cloned.1.call-update) | async-done | bytes 2097168 | tf_op jit(solution)/shard_map/all_gather | solution.py:72
  312.5 4.4 %fusion.32 = f32[8,1024,128]{2,1,0:T(8,128)} fusion(bf16[1024,8,128]{0,2,1:T(8,128)(2,1)} %bitcast.85, bf16[128,1024]{1,0:T(8,128)(2,1)S(1)} %copy-done.5), kind=kOutput, calls=%fused_computation.32 | convolution fusion | flops 268435456 | bytes 6553600 | tf_op jit(solution)/shard_map/qhd,khd->hqk/dot_general | solution.py:81
  316.8 44.9 %all-gather.13.cloned.1.call-done = bf16[1024,1024]{1,0:T(8,128)(2,1)} async-done(((bf16[128,1024]{1,0:T(8,128)(2,1)}), bf16[1024,1024]{1,0:T(8,128)(2,1)}) %all-gather.13.cloned.1.call-update) | async-done | bytes 2097168 | tf_op jit(solution)/shard_map/all_gather | solution.py:43
  361.7 4.1 fusion.17
  365.9 0.4 multiply_reduce_fusion
  366.4 5.0 %fusion.20 = f32[128,8,128]{0,2,1:T(8,128)S(1)} fusion(bf16[1024,8,128]{0,2,1:T(8,128)(2,1)S(1)} %bitcast.88, f32[8,128,1024]{2,1,0:T(8,128)} %copy-done, f32[8,128]{1,0:T(8,128)S(1)} %log_add_fusion, pred[128,1024]{1,0:T(8,128)(4,1)S(1)} %broadcast_compare_fusion.1, bf16[1024,1024]{1,0:T(8,128)(2,1)} %all-gather.13.cloned.1.call-done, ...), kind=kOutput, calls=%fused_computation.22 | convolution fusion | flops 542113792 | bytes 9310208 | tf_op jit(solution)/shard_map/hqk,khd->hqd/dot_general | solution.py:59
  371.4 3.4 fusion.28
  374.8 0.9 copy.25
  375.6 31.3 %all_gather.32 = f32[1024,8]{0,1:T(8,128)S(1)} all-gather(f32[128,8]{0,1:T(8,128)S(1)} %copy.37), channel_id=1, replica_groups=mesh['ctx'=8,'head'=4] {'ctx'}, dimensions={0}, use_global_device_ids=true | all-gather | bytes 36864 | tf_op jit(solution)/shard_map/all_gather | solution.py:70
  406.9 5.4 %all-gather.17.cloned.1.call-done = bf16[1024,1024]{1,0:T(8,128)(2,1)} async-done(((bf16[128,1024]{1,0:T(8,128)(2,1)}), bf16[1024,1024]{1,0:T(8,128)(2,1)}) %all-gather.17.cloned.1.call-update) | async-done | bytes 2097168 | tf_op jit(solution)/shard_map/all_gather | solution.py:73
  412.4 3.9 copy.42
  416.3 3.9 fusion.29
  420.2 0.9 copy.27
  421.0 5.9 %fusion.27 = bf16[8,128,128]{1,2,0:T(8,128)(2,1)S(1)} fusion(bf16[1024,8,128]{0,2,1:T(8,128)(2,1)S(1)} %bitcast.86, f32[8,1024,128]{2,1,0:T(8,128)} %fusion.32, bf16[1024,8,128]{0,2,1:T(8,128)(2,1)} %bitcast.91, bf16[128,8,128]{0,2,1:T(8,128)(2,1)S(1)} %bitcast.93, f32[8,1024]{1,0:T(8,128)S(1)} %bitcast.99, f32[8,1024]{1,0:T(8,128)S(1)} %bitcast.98, ...), kind=kOutput, calls=%fused_computation.27 | convolution fusion | flops 543424512 | bytes 9109504 | tf_op jit(solution)/shard_map/hqk,qhd->hkd/dot_general | solution.py:93
  426.9 0.9 copy.26
  (26 shorter events, 0.4 us)
Async XLA Ops:
  7.2 7.0 %copy-start.6 = (s32[1024]{0:T(1024)S(1)}, s32[1024]{0:T(1024)}, u32[]{:S(2)}) copy-start(s32[1024]{0:T(1024)} %param.11) | copy-start | bytes 12292
  7.2 24.8 %all-gather.9.cloned.1.call-start = ((), (), s32[]{:S(2)}) async-start(), calls=%async_computation.1 | async-start | bytes 1966080 | tf_op jit(solution)/shard_map/all_gather | solution.py:16
  7.9 202.3 %all-gather.11.cloned.1.call-start = ((), (), s32[]{:S(2)}) async-start(), calls=%async_computation.2 | async-start | bytes 14155776 | tf_op jit(solution)/shard_map/all_gather | solution.py:19
  8.7 252.8 %all-gather.7.cloned.1.call-start = ((), (), s32[]{:S(2)}) async-start(), calls=%async_computation | async-start | bytes 2359296 | tf_op jit(solution)/shard_map/all_gather | solution.py:42
  10.5 301.9 %all-gather.15.cloned.1.call-start = ((), (), s32[]{:S(2)}) async-start(), calls=%async_computation.4 | async-start | bytes 2359296 | tf_op jit(solution)/shard_map/all_gather | solution.py:72
  12.4 349.4 %all-gather.13.cloned.1.call-start = ((), (), s32[]{:S(2)}) async-start(), calls=%async_computation.3 | async-start | bytes 2359296 | tf_op jit(solution)/shard_map/all_gather | solution.py:43
  13.0 399.4 %all-gather.17.cloned.1.call-start = ((), (), s32[]{:S(2)}) async-start(), calls=%async_computation.5 | async-start | bytes 2359296 | tf_op jit(solution)/shard_map/all_gather | solution.py:73
  14.4 247.0 %copy-start.4 = (bf16[128,1024]{1,0:T(8,128)(2,1)S(1)}, bf16[128,1024]{1,0:T(8,128)(2,1)}, u32[]{:S(2)}) copy-start(bf16[128,1024]{1,0:T(8,128)(2,1)} %param.6) | copy-start | bytes 786436
  261.4 51.0 %copy-start.5 = (bf16[128,1024]{1,0:T(8,128)(2,1)S(1)}, bf16[128,1024]{1,0:T(8,128)(2,1)}, u32[]{:S(2)}) copy-start(bf16[128,1024]{1,0:T(8,128)(2,1)} %param.7) | copy-start | bytes 786436
  264.2 2.0 copy-start
  316.8 49.0 %copy-start.1 = (bf16[128,1024]{1,0:T(8,128)(2,1)S(1)}, bf16[128,1024]{1,0:T(8,128)(2,1)}, u32[]{:S(2)}) copy-start(bf16[128,1024]{1,0:T(8,128)(2,1)} %convolution_convert_fusion) | copy-start | bytes 786436
  316.8 49.5 %copy-start.3 = (bf16[1024,1024]{0,1:T(8,128)(2,1)S(1)}, bf16[1024,1024]{0,1:T(8,128)(2,1)}, u32[]{:S(2)}) copy-start(bf16[1024,1024]{0,1:T(8,128)(2,1)} %all-gather.7.cloned.1.call-done) | copy-start | bytes 6291460
  416.3 4.7 %copy-start.2 = (bf16[1024,1024]{0,1:T(8,128)(2,1)S(1)}, bf16[1024,1024]{0,1:T(8,128)(2,1)}, u32[]{:S(2)}) copy-start(bf16[1024,1024]{0,1:T(8,128)(2,1)} %all-gather.15.cloned.1.call-done) | copy-start | bytes 6291460
Sparse Core Ops, SparseCore 0:
  9.5 22.3 all-gather.8
  34.1 176.0 all-gather.10
  212.9 48.5 all-gather.6
  263.9 48.4 all-gather.14
  314.4 47.2 all-gather.12
  364.3 48.0 all-gather.16
where the time goes:
time: 435 us
  waiting for transfers between devices  305 us (70%)
  blocking collectives  62.4 us (14%)
  matrix products  36.9 us (8%)
  between operations  14.2 us (3%)
  local copies, waits for them, and re-layouts  13.3 us (3%)
    all_gather x1, waiting for transfers between devices, body(): lax.all_gather(out_weight, 'ctx', axis=0, tiled=True)  178 us
    all_gather x1, waiting for transfers between devices, body(): value_piece = lax.all_gather(value_rows, 'ctx', axis=0, tiled=True)  44.9 us
    all_gather x1, waiting for transfers between devices, body(): key_piece = lax.all_gather(key_rows, 'ctx', axis=0, tiled=True)  43.4 us
    all_gather x1, blocking collectives, body(): lax.all_gather(delta.T, 'ctx', axis=0, tiled=True)  31.3 us
    all_gather x1, blocking collectives, body(): lax.all_gather(log_total.T, 'ctx', axis=0, tiled=True)  31.1 us
    all_gather x1, waiting for transfers between devices, body(): upstream_full = lax.all_gather(upstream, 'head', axis=1, tiled=True)  17.5 us
    all_gather x1, waiting for transfers between devices, body(): query_piece = lax.all_gather(queries, 'ctx', axis=0, tiled=True)  13.9 us
  transfers between devices with their start and end apart: 6, of which 6 were waited for; matrix products, arithmetic and copies ran while one was open for 8% of the time, Pallas kernels for 0%

commit v1 on v0

--- a/solution.py
+++ b/solution.py
@@ -39,8 +39,11 @@
     run_sum = jnp.sum(weights, axis=2)
     run_max, run_sum = (new_max, run_sum)
     log_total = run_max + jnp.log(run_sum)
-    key_piece = lax.all_gather(key_rows, "ctx", axis=0, tiled=True)
-    value_piece = lax.all_gather(value_rows, "ctx", axis=0, tiled=True)
+    key_piece, value_piece = jnp.split(
+        lax.all_gather(jnp.concatenate([key_rows, value_rows], axis=1), "ctx", axis=0, tiled=True),
+        [key_rows.shape[1]],
+        axis=1,
+    )
     piece_rows = key_piece.shape[0]
     piece_ids = group_ids
     key_block = key_piece.reshape(piece_rows, heads_dev, HDIM)

time: 435 us -> 460 us (1.057)
  waiting for transfers between devices: 305 us -> 326 us
    all_gather x1, waiting for transfers between devices: 44.9 us -> 70.5 us  [body(): lax.all_gather(jnp.concatenate([key_rows, value_rows], axis=1), 'ctx', ax...]
  transfers between devices with their start and end apart: 6 -> 6, of which waited for: 6 -> 6; matrix products, arithmetic and copies ran while one was open for 8% -> 9% of each run, Pallas kernels for 0% -> 0%
where the time goes in v1:
time: 460 us
  waiting for transfers between devices  326 us (71%)
  blocking collectives  62 us (13%)
  matrix products  37 us (8%)
  local copies, waits for them, and re-layouts  14.5 us (3%)
  between operations  14.3 us (3%)
  other arithmetic  5.98 us (1%)
    all_gather x1, waiting for transfers between devices, body(): lax.all_gather(out_weight, 'ctx', axis=0, tiled=True)  178 us
    all_gather x1, waiting for transfers between devices, body(): lax.all_gather(jnp.concatenate([key_rows, value_rows], axis=1), 'ctx', ax...  70.5 us
    all_gather x1, waiting for transfers between devices, body(): key_piece = lax.all_gather(key_rows, 'ctx', axis=0, tiled=True)  47.7 us
    all_gather x1, blocking collectives, body(): lax.all_gather(log_total.T, 'ctx', axis=0, tiled=True)  31.1 us
    all_gather x1, blocking collectives, body(): lax.all_gather(delta.T, 'ctx', axis=0, tiled=True)  31 us
    all_gather x1, waiting for transfers between devices, body(): upstream_full = lax.all_gather(upstream, 'head', axis=1, tiled=True)  14.8 us
    all_gather x1, waiting for transfers between devices, body(): query_piece = lax.all_gather(queries, 'ctx', axis=0, tiled=True)  9.28 us
  transfers between devices with their start and end apart: 6, of which 6 were waited for; matrix products, arithmetic and copies ran while one was open for 9% of the time, Pallas kernels for 0%

profile of v1, /device:TPU:0, one launch (start us, length us, event | category | flops | bytes accessed | tf_op | source)
XLA Modules:
  0.0 459.9 jit_solution(8275290161416728958)
XLA Ops:
  7.2 1.8 copy.22
  9.1 0.7 all-gather.11.cloned.1.call-update
  9.8 0.7 all-gather.13.cloned.1.call-update
  10.6 1.8 copy.32
  12.5 1.1 copy.23
  13.6 1.8 pad_maximum_fusion
  15.5 0.2 broadcast_compare_fusion.1
  16.0 47.7 %all-gather.9.cloned.1.call-done = bf16[1024,1024]{0,1:T(8,128)(2,1)} async-done(((bf16[128,1024]{0,1:T(8,128)(2,1)}), bf16[1024,1024]{0,1:T(8,128)(2,1)}) %all-gather.9.cloned.1.call-update) | async-done | bytes 2097168 | tf_op jit(solution)/shard_map/all_gather | solution.py:27
  63.7 4.6 fusion
  68.3 14.8 %all-gather.11.cloned.1.call-done = bf16[128,6144]{1,0:T(8,128)(2,1)} async-done(((bf16[128,1536]{1,0:T(8,128)(2,1)}), bf16[128,6144]{1,0:T(8,128)(2,1)}) %all-gather.11.cloned.1.call-update) | async-done | bytes 1572880 | tf_op jit(solution)/shard_map/all_gather | solution.py:16
  83.1 178.3 %all-gather.13.cloned.1.call-done = bf16[6144,1024]{1,0:T(8,128)(2,1)} async-done(((bf16[768,1024]{1,0:T(8,128)(2,1)}), bf16[6144,1024]{1,0:T(8,128)(2,1)}) %all-gather.13.cloned.1.call-update) | async-done | bytes 12582928 | tf_op jit(solution)/shard_map/all_gather | solution.py:19
  261.5 7.6 %convolution_convert_fusion = bf16[128,1024]{1,0:T(8,128)(2,1)} fusion(bf16[128,6144]{1,0:T(8,128)(2,1)} %all-gather.11.cloned.1.call-done, bf16[6144,1024]{1,0:T(8,128)(2,1)} %all-gather.13.cloned.1.call-done), kind=kOutput, calls=%fused_computation.24 | convolution fusion | flops 1610743808 | bytes 14417920 | tf_op jit(solution)/shard_map/dot_general | solution.py:17
  269.1 3.4 select_reduce_fusion
  272.4 31.1 %all_gather.29 = f32[1024,8]{0,1:T(8,128)S(1)} all-gather(f32[128,8]{0,1:T(8,128)S(1)} %bitcast.106), channel_id=1, replica_groups=mesh['ctx'=8,'head'=4] {'ctx'}, dimensions={0}, use_global_device_ids=true | all-gather | bytes 36864 | tf_op jit(solution)/shard_map/all_gather | solution.py:72
  303.5 9.3 %all-gather.15.cloned.1.call-done = bf16[1024,1024]{0,1:T(8,128)(2,1)} async-done(((bf16[128,1024]{0,1:T(8,128)(2,1)}), bf16[1024,1024]{0,1:T(8,128)(2,1)}) %all-gather.15.cloned.1.call-update) | async-done | bytes 2097168 | tf_op jit(solution)/shard_map/all_gather | solution.py:75
  312.8 4.4 fusion.21
  317.1 70.5 %all-gather.7.cloned.1.call-done = bf16[1024,2048]{0,1:T(8,128)(2,1)} async-done(((bf16[128,2048]{0,1:T(8,128)(2,1)}), bf16[1024,2048]{0,1:T(8,128)(2,1)}) %all-gather.7.cloned.1.call-update) | async-done | bytes 4194320 | tf_op jit(solution)/shard_map/all_gather | solution.py:43
  387.6 2.7 fusion.42
  390.3 0.8 fusion.30
  391.1 1.4 convolution_bitcast_fusion.1
  392.6 0.5 copy-done
  393.1 0.4 multiply_reduce_fusion
  393.5 5.0 %fusion.11 = f32[128,8,128]{0,2,1:T(8,128)S(1)} fusion(bf16[1024,8,128]{0,2,1:T(8,128)(2,1)S(1)} %bitcast.88, f32[8,1024,128]{2,1,0:T(8,128)} %copy-done, bf16[1024,8,128]{0,2,1:T(8,128)(2,1)} %bitcast.97, f32[8,128]{1,0:T(8,128)S(1)} %log_add_fusion, pred[128,1024]{0,1:T(8,128)(4,1)S(1)} %broadcast_compare_fusion.1, bf16[128,1024]{1,0:T(8,128)(2,1)S(1)} %copy-done.1), kind=kOutput, calls=%fused_computation.18 | convolution fusion | flops 542113792 | bytes 9310208 | tf_op jit(solution)/shard_map/hqk,khd->hqd/dot_general | solution.py:62
  398.5 3.5 fusion.17
  402.0 0.9 copy.36
  402.9 31.0 %all_gather.31 = f32[1024,8]{0,1:T(8,128)S(1)} all-gather(f32[128,8]{0,1:T(8,128)S(1)} %copy.49), channel_id=1, replica_groups=mesh['ctx'=8,'head'=4] {'ctx'}, dimensions={0}, use_global_device_ids=true | all-gather | bytes 36864 | tf_op jit(solution)/shard_map/all_gather | solution.py:73
  433.9 3.8 all-gather.17.cloned.1.call-done
  437.6 3.9 copy.55
  441.6 3.9 fusion.18
  445.4 0.9 copy.38
  446.3 5.9 %fusion.16 = bf16[8,128,128]{1,2,0:T(8,128)(2,1)S(1)} fusion(bf16[1024,8,128]{0,2,1:T(8,128)(2,1)S(1)} %bitcast.92, f32[8,1024,128]{2,1,0:T(8,128)} %fusion.21, bf16[1024,8,128]{0,2,1:T(8,128)(2,1)} %bitcast.95, bf16[128,8,128]{0,2,1:T(8,128)(2,1)S(1)} %bitcast.99, f32[8,1024]{1,0:T(8,128)S(1)} %bitcast.105, f32[8,1024]{1,0:T(8,128)S(1)} %bitcast.104, ...), kind=kOutput, calls=%fused_computation.23 | convolution fusion | flops 543424512 | bytes 9109504 | tf_op jit(solution)/shard_map/hqk,qhd->hkd/dot_general | solution.py:96
  452.2 0.9 copy.37
  (29 shorter events, 0.7 us)
Async XLA Ops:
  7.2 56.6 %copy-start.2 = (bf16[128,1024]{1,0:T(8,128)(2,1)S(1)}, bf16[128,1024]{1,0:T(8,128)(2,1)}, u32[]{:S(2)}) copy-start(bf16[128,1024]{1,0:T(8,128)(2,1)} %param.6) | copy-start | bytes 786436
  7.2 8.3 %copy-start.6 = (s32[1024]{0:T(1024)S(1)}, s32[1024]{0:T(1024)}, u32[]{:S(2)}) copy-start(s32[1024]{0:T(1024)} %param.11) | copy-start | bytes 12292
  7.2 56.5 %all-gather.9.cloned.1.call-start = ((), (), s32[]{:S(2)}) async-start(), calls=%async_computation.1 | async-start | bytes 2359296 | tf_op jit(solution)/shard_map/all_gather | solution.py:27
  9.0 74.1 %all-gather.11.cloned.1.call-start = ((), (), s32[]{:S(2)}) async-start(), calls=%async_computation.2 | async-start | bytes 1966080 | tf_op jit(solution)/shard_map/all_gather | solution.py:16
  9.8 251.7 %all-gather.13.cloned.1.call-start = ((), (), s32[]{:S(2)}) async-start(), calls=%async_computation.3 | async-start | bytes 14155776 | tf_op jit(solution)/shard_map/all_gather | solution.py:19
  10.5 302.2 %all-gather.15.cloned.1.call-start = ((), (), s32[]{:S(2)}) async-start(), calls=%async_computation.4 | async-start | bytes 2359296 | tf_op jit(solution)/shard_map/all_gather | solution.py:75
  12.4 375.2 %all-gather.7.cloned.1.call-start = ((), (), s32[]{:S(2)}) async-start(), calls=%async_computation | async-start | bytes 4718592 | tf_op jit(solution)/shard_map/all_gather | solution.py:43
  15.4 422.2 %all-gather.17.cloned.1.call-start = ((), (), s32[]{:S(2)}) async-start(), calls=%async_computation.5 | async-start | bytes 2359296 | tf_op jit(solution)/shard_map/all_gather | solution.py:76
  269.0 43.8 %copy-start.5 = (bf16[128,1024]{1,0:T(8,128)(2,1)S(1)}, bf16[128,1024]{1,0:T(8,128)(2,1)}, u32[]{:S(2)}) copy-start(bf16[128,1024]{1,0:T(8,128)(2,1)} %param.7) | copy-start | bytes 786436
  390.3 2.3 copy-start.4
  391.1 2.0 copy-start
  391.1 1.4 copy-start.1
  441.6 4.7 %copy-start.3 = (bf16[1024,1024]{0,1:T(8,128)(2,1)S(1)}, bf16[1024,1024]{0,1:T(8,128)(2,1)}, u32[]{:S(2)}) copy-start(bf16[1024,1024]{0,1:T(8,128)(2,1)} %all-gather.15.cloned.1.call-done) | copy-start | bytes 6291460
Sparse Core Ops, SparseCore 0:
  10.6 53.0 all-gather.8
  65.3 17.8 all-gather.10
  85.3 176.0 all-gather.12
  263.9 48.8 all-gather.14
  314.7 72.8 all-gather.6
  390.2 47.4 all-gather.16
